TPU v7x, 32 devices: a whole 2x2x4 slice. The times are simulated.
32 devices in a mesh: seq: 8 (over z, y), tp: 4 (over x, core).
Axes of the slice: x: 2, y: 2, z: 4, core: 2. Of those that a mesh axis runs over, the one named last changes fastest.
Arguments:
- tokens: bfloat16 [8192, 1152], P('seq', 'tp'), may hold values from -6 to 6
- out_grad: bfloat16 [8192, 1152], P('seq', 'tp'), may hold values from -6 to 6
- route_mask: int32 [8192], P('seq'), may hold values from 0 to 1, as said below
- kept_counts: int32 [32], replicated, may hold values from 64 to 192, as said below
- labels: int32 [32], replicated, may hold values from 0 to 1000
- timesteps: int32 [32], replicated, may hold values from 0 to 999
- class_table: bfloat16 [1001, 1152], replicated, may hold values from -6 to 6
- ada_weight: bfloat16 [1152, 6, 1152], P(None, None, 'tp'), may hold values from -0.1875 to 0.1875
- ada_bias: bfloat16 [6, 1152], P(None, 'tp'), may hold values from -2 to 2
- qkv_weight: bfloat16 [1152, 3, 1152], P(None, None, 'tp'), may hold values from -0.1875 to 0.1875
- qv_bias: bfloat16 [2, 1152], P(None, 'tp'), may hold values from -2 to 2
- proj_weight: bfloat16 [1152, 1152], P('tp'), may hold values from -0.5 to 0.5
- proj_bias: bfloat16 [1152], P('tp'), may hold values from -2 to 2
- hidden_weight: bfloat16 [1152, 4608], P(None, 'tp'), may hold values from -0.1875 to 0.1875
- hidden_bias: bfloat16 [4608], P('tp'), may hold values from -2 to 2
- output_weight: bfloat16 [4608, 1152], P('tp'), may hold values from -0.09375 to 0.09375
- output_bias: bfloat16 [1152], P('tp'), may hold values from -2 to 2
Outputs:
- output: bfloat16 [8192, 1152], P('seq', 'tp')
- tokens_grad: bfloat16 [8192, 1152], P('seq', 'tp')
- class_grad: float32 [1001, 1152], P(None, 'seq')
- ada_weight_grad: float32 [1152, 6, 1152], P('seq', None, 'tp')
- ada_bias_grad: float32 [6, 1152], P(None, 'tp')
- qkv_weight_grad: float32 [1152, 3, 1152], P('seq', None, 'tp')
- qv_bias_grad: float32 [2, 1152], P(None, 'tp')
- proj_weight_grad: float32 [1152, 1152], P('tp', 'seq')
- proj_bias_grad: float32 [1152], P('tp')
- hidden_weight_grad: float32 [1152, 4608], P('seq', 'tp')
- hidden_bias_grad: float32 [4608], P('tp')
- output_weight_grad: float32 [4608, 1152], P('tp', 'seq')
- output_bias_grad: float32 [1152], P('tp')
Inputs may be any that keep to these rules, and one draw needn't show every extreme that they name: route_mask keeps exactly kept_counts[i] of the 256 tokens of image i. The kept tokens of all images number 512 * 8; the kept tokens of the first j * 4 images exceed j * 512 by 0 to 128 for every j, by exactly 128 for some j, and by 0 at the end. Every aligned block of 4 images has one image with 192 kept tokens. `route_mask`: consistent with kept_counts.
All inputs are finite; a program needn't handle non-finite values.
Results may differ from a plain program's by a relative error of at most 0.025.
The roundings to bfloat16 on the way count: a program that leaves them out, or rounds other values in their place, can miss the bound.
Values may be sent and summed in bfloat16 or wider, within the bound.
A program may use at most 192 MiB of HBM per device.

v0:
```python
import math
import jax
import jax.numpy as jnp
from jax import lax
from jax.sharding import PartitionSpec as P

HEAD_DIM = 72
IMG_DEV = 4
ROWS = 640
NORM_EPS = 1e-06
HIGHEST = lax.Precision.HIGHEST


def exact_dot(left_mat, right_mat):
    return jnp.dot(left_mat, right_mat, precision=HIGHEST, preferred_element_type=jnp.float32)


def time_embed(step_ids, model_width):
    half_width = model_width // 2
    frequency = jnp.exp(-math.log(10000.0) * jnp.arange(half_width, dtype=jnp.float32) / half_width)
    angles = step_ids.astype(jnp.float32)[:, None] * frequency[None, :]
    return jnp.concatenate([jnp.cos(angles), jnp.sin(angles)], axis=1)


def norm_rows(values):
    centered = values - jnp.mean(values, axis=1, keepdims=True)
    inverse = lax.rsqrt(jnp.mean(centered * centered, axis=1, keepdims=True) + NORM_EPS)
    return (centered * inverse, inverse)


def gelu_tanh(values):
    return jax.nn.gelu(values, approximate=True)


def local(
    tokens,
    out_grad,
    route_mask,
    kept_counts,
    labels,
    timesteps,
    class_table,
    ada_weight,
    ada_bias,
    qkv_weight,
    qv_bias,
    proj_weight,
    proj_bias,
    hidden_weight,
    hidden_bias,
    output_weight,
    output_bias,
):
    f32, bf16 = (jnp.float32, jnp.bfloat16)
    seq_index = lax.axis_index("seq")
    tp_index = lax.axis_index("tp")
    seq_size = lax.axis_size("seq")
    col_local = tokens.shape[1]
    model_width = class_table.shape[1]
    head_cols = qkv_weight.shape[2]
    heads_local = head_cols // HEAD_DIM
    slice_width = model_width // seq_size
    images = kept_counts.shape[0]
    scale_factor = HEAD_DIM ** (-0.5)
    col_start = tp_index * col_local
    first_image = seq_index * IMG_DEV
    own_counts = lax.dynamic_slice_in_dim(kept_counts, first_image, IMG_DEV)
    own_ends = jnp.cumsum(own_counts)
    rank = jnp.where(route_mask > 0, jnp.cumsum(route_mask) - 1, -1)
    row_ids = jnp.arange(ROWS, dtype=jnp.int32)
    place = (rank[None, :] == row_ids[:, None]).astype(bf16)
    row_image = jnp.sum((own_ends[None, :] <= row_ids[:, None]).astype(jnp.int32), axis=1)
    row_onehot = (row_image[:, None] == jnp.arange(IMG_DEV, dtype=jnp.int32)[None, :]).astype(f32)

    def whole_rows(part_rows):
        return lax.all_gather(part_rows, "tp", axis=1, tiled=True)

    def column_sum(part_rows):
        return lax.psum_scatter(
            part_rows.astype(bf16), "tp", scatter_dimension=1, tiled=True
        ).astype(f32)

    def own_cols(full_rows):
        return lax.dynamic_slice_in_dim(full_rows, col_start, col_local, 1)

    def reinsert(rows_new, initial):
        placed = jnp.einsum("rt,rc->tc", place, rows_new, preferred_element_type=f32).astype(bf16)
        return jnp.where(route_mask[:, None] > 0, placed, initial)

    label_hot = (
        labels[:, None] == jnp.arange(class_table.shape[0], dtype=jnp.int32)[None, :]
    ).astype(bf16)
    condition = jnp.dot(label_hot, class_table, preferred_element_type=f32) + time_embed(
        timesteps, model_width
    )
    cond_low = jax.nn.silu(condition).astype(bf16)
    cond_own = lax.dynamic_slice_in_dim(cond_low, first_image, IMG_DEV)
    mod_own = (
        jnp.einsum("wd,dcf->wcf", cond_own, ada_weight, preferred_element_type=f32)
        + ada_bias.astype(f32)[None]
    )
    mod_full = lax.all_gather(mod_own, "tp", axis=2, tiled=True)

    def row_full(stretch_id):
        return exact_dot(row_onehot, mod_full[:, stretch_id, :])

    def row_own(stretch_id):
        return exact_dot(row_onehot, mod_own[:, stretch_id, :])

    def input_grads(partial_rows, normed, inverse, scale):
        own_grad = column_sum(partial_rows)
        normed_own = own_cols(normed)
        scaled_grad = own_grad * (1.0 + own_cols(scale))
        mean_grad, mean_cross = lax.psum(
            (
                jnp.sum(scaled_grad, axis=1, keepdims=True) / model_width,
                jnp.sum(scaled_grad * normed_own, axis=1, keepdims=True) / model_width,
            ),
            "tp",
        )
        return (
            own_grad,
            own_grad * normed_own,
            inverse * (scaled_grad - mean_grad - normed_own * mean_cross),
        )

    picked = jnp.dot(place, jnp.concatenate([tokens, out_grad], axis=1), preferred_element_type=f32)
    rows_in = picked[:, :col_local].astype(bf16)
    grad_rows = picked[:, col_local:]
    gate_one = row_own(2)
    gate_two = row_own(5)
    mlp_grad = (grad_rows * gate_two).astype(bf16)
    full_in = whole_rows(rows_in).astype(f32)
    mlp_grad_full = whole_rows(mlp_grad)
    normed_one, inverse_one = norm_rows(full_in)
    scale_one = row_full(1)
    branch_one = (normed_one * (1.0 + scale_one) + row_full(0)).astype(bf16)
    qkv_bias = jnp.stack([qv_bias[0], jnp.zeros_like(qv_bias[0]), qv_bias[1]]).astype(f32)
    qkv_rows = (
        jnp.einsum("rd,dcf->rcf", branch_one, qkv_weight, preferred_element_type=f32)
        + qkv_bias[None]
    ).astype(bf16)
    query_all, key_all, value_all = (
        qkv_rows[:, part].reshape(ROWS, heads_local, HEAD_DIM) for part in range(3)
    )
    same_image = row_image[:, None] == row_image[None, :]
    raw = jnp.einsum("qhe,khe->hqk", query_all, key_all, preferred_element_type=f32) * scale_factor
    masked = jnp.where(same_image[None], raw, -1e30)
    top_score = jnp.max(masked, axis=2, keepdims=True)
    exp_scores = jnp.exp(masked - top_score)
    attn_probs = exp_scores / jnp.sum(exp_scores, axis=2, keepdims=True)
    probs_low = attn_probs.astype(bf16)
    attended = (
        jnp.einsum("hqk,khe->qhe", probs_low, value_all, preferred_element_type=f32)
        .reshape(ROWS, head_cols)
        .astype(bf16)
    )
    attn_out = column_sum(
        jnp.dot(attended, proj_weight, preferred_element_type=f32)
    ) + proj_bias.astype(f32)
    middle = rows_in.astype(f32) + gate_one * attn_out
    middle_full = whole_rows(middle.astype(bf16)).astype(f32)
    normed_two, inverse_two = norm_rows(middle_full)
    scale_two = row_full(4)
    branch_two = (normed_two * (1.0 + scale_two) + row_full(3)).astype(bf16)
    pre_act = jnp.dot(branch_two, hidden_weight, preferred_element_type=f32) + hidden_bias.astype(
        f32
    )
    act_low = gelu_tanh(pre_act).astype(bf16)
    mlp_out = column_sum(
        jnp.dot(act_low, output_weight, preferred_element_type=f32)
    ) + output_bias.astype(f32)
    final_rows = middle + gate_two * mlp_out
    output = reinsert(final_rows.astype(bf16), tokens)
    gate_two_rows = grad_rows * mlp_out
    output_bias_term = jnp.sum(mlp_grad, axis=0, dtype=f32)
    output_weight_term = jnp.einsum(
        "rf,rd->fd", act_low, mlp_grad_full, preferred_element_type=f32
    ).astype(bf16)
    act_grad = jnp.einsum("rd,fd->rf", mlp_grad_full, output_weight, preferred_element_type=f32)
    gelu_pull = jax.vjp(gelu_tanh, pre_act)[1]
    pre_grad = gelu_pull(act_grad)[0].astype(bf16)
    hidden_bias_term = jnp.sum(pre_grad, axis=0, dtype=f32)
    hidden_weight_term = jnp.einsum(
        "rd,rf->df", branch_two, pre_grad, preferred_element_type=f32
    ).astype(bf16)
    two_partial = jnp.einsum("rf,df->rd", pre_grad, hidden_weight, preferred_element_type=f32)
    shift_two_grad, scale_two_grad, two_norm_grad = input_grads(
        two_partial, normed_two, inverse_two, scale_two
    )
    middle_grad = grad_rows + two_norm_grad
    gate_one_rows = middle_grad * attn_out
    attn_grad = (middle_grad * gate_one).astype(bf16)
    proj_bias_term = jnp.sum(attn_grad, axis=0, dtype=f32)
    attn_grad_full = whole_rows(attn_grad)
    proj_weight_term = jnp.einsum(
        "rf,rd->fd", attended, attn_grad_full, preferred_element_type=f32
    ).astype(bf16)
    attended_grad = (
        jnp.einsum("rd,fd->rf", attn_grad_full, proj_weight, preferred_element_type=f32)
        .astype(bf16)
        .reshape(ROWS, heads_local, HEAD_DIM)
    )
    value_term = jnp.einsum("hqk,qhe->khe", probs_low, attended_grad, preferred_element_type=f32)
    prob_grad = jnp.einsum("qhe,khe->hqk", attended_grad, value_all, preferred_element_type=f32)
    row_dot = jnp.sum(attn_probs * prob_grad, axis=2, keepdims=True)
    score_grad = (attn_probs * (prob_grad - row_dot)).astype(bf16)
    query_term = (
        jnp.einsum("hqk,khe->qhe", score_grad, key_all, preferred_element_type=f32) * scale_factor
    )
    key_term = (
        jnp.einsum("hqk,qhe->khe", score_grad, query_all, preferred_element_type=f32) * scale_factor
    )
    qkv_grad = (
        jnp.stack([query_term, key_term, value_term], axis=1)
        .reshape(ROWS, 3, head_cols)
        .astype(bf16)
    )
    qkv_sums = jnp.sum(qkv_grad, axis=0, dtype=f32)
    qkv_weight_term = jnp.einsum(
        "rd,rcf->dcf", branch_one, qkv_grad, preferred_element_type=f32
    ).astype(bf16)
    one_partial = jnp.einsum("rcf,dcf->rd", qkv_grad, qkv_weight, preferred_element_type=f32)
    shift_one_grad, scale_one_grad, one_norm_grad = input_grads(
        one_partial, normed_one, inverse_one, scale_one
    )
    in_grad = middle_grad + one_norm_grad
    tokens_grad = reinsert(in_grad.astype(bf16), out_grad)
    per_row = jnp.concatenate(
        [
            shift_one_grad,
            scale_one_grad,
            gate_one_rows,
            shift_two_grad,
            scale_two_grad,
            gate_two_rows,
        ],
        axis=1,
    )
    mod_grad = jnp.einsum(
        "rw,rf->wf", row_onehot, per_row, precision=HIGHEST, preferred_element_type=f32
    )
    small = jnp.concatenate(
        [
            mod_grad.reshape(-1),
            qkv_sums[0],
            qkv_sums[2],
            proj_bias_term,
            hidden_bias_term,
            output_bias_term,
        ]
    )
    small_all = lax.all_gather(small, "seq", axis=0)
    mod_size = mod_grad.size
    mod_all = small_all[:, :mod_size].reshape(images, 6, col_local)
    bias_sums = jnp.sum(small_all[:, mod_size:], axis=0)
    ada_bias_grad = jnp.sum(mod_all, axis=0)
    qv_bias_grad = bias_sums[: 2 * col_local].reshape(2, col_local)
    at = 2 * col_local
    proj_bias_grad = bias_sums[at : at + col_local]
    at += col_local
    hidden_bias_grad = bias_sums[at : at + hidden_bias.shape[0]]
    at += hidden_bias.shape[0]
    output_bias_grad = bias_sums[at:]
    width_start = seq_index * slice_width
    cond_cols = lax.dynamic_slice_in_dim(condition, width_start, slice_width, 1)
    low_cols = lax.dynamic_slice_in_dim(cond_low, width_start, slice_width, 1)
    ada_weight_grad = jnp.einsum(
        "wd,wcf->dcf", low_cols.astype(f32), mod_all, precision=HIGHEST, preferred_element_type=f32
    )
    ada_rows = lax.dynamic_slice_in_dim(ada_weight, width_start, slice_width, 0)
    cond_grad = lax.psum(
        jnp.einsum(
            "wcf,dcf->wd",
            mod_all,
            ada_rows.astype(f32),
            precision=HIGHEST,
            preferred_element_type=f32,
        ),
        "tp",
    )
    silu_pull = jax.vjp(jax.nn.silu, cond_cols)[1]
    class_grad = jnp.einsum(
        "wc,wd->cd",
        label_hot.astype(f32),
        silu_pull(cond_grad)[0],
        precision=HIGHEST,
        preferred_element_type=f32,
    )
    qkv_weight_grad, proj_weight_grad, hidden_weight_grad, output_weight_grad = (
        lax.psum_scatter(qkv_weight_term, "seq", scatter_dimension=0, tiled=True).astype(f32),
        lax.psum_scatter(proj_weight_term, "seq", scatter_dimension=1, tiled=True).astype(f32),
        lax.psum_scatter(hidden_weight_term, "seq", scatter_dimension=0, tiled=True).astype(f32),
        lax.psum_scatter(output_weight_term, "seq", scatter_dimension=1, tiled=True).astype(f32),
    )
    return (
        output,
        tokens_grad,
        class_grad,
        ada_weight_grad,
        ada_bias_grad,
        qkv_weight_grad,
        qv_bias_grad,
        proj_weight_grad,
        proj_bias_grad,
        hidden_weight_grad,
        hidden_bias_grad,
        output_weight_grad,
        output_bias_grad,
    )


def solution(mesh):
    return jax.shard_map(
        local,
        mesh=mesh,
        in_specs=(
            P("seq", "tp"),
            P("seq", "tp"),
            P("seq"),
            P(),
            P(),
            P(),
            P(),
            P(None, None, "tp"),
            P(None, "tp"),
            P(None, None, "tp"),
            P(None, "tp"),
            P("tp", None),
            P("tp"),
            P(None, "tp"),
            P("tp"),
            P("tp", None),
            P("tp"),
        ),
        out_specs=(
            P("seq", "tp"),
            P("seq", "tp"),
            P(None, "seq"),
            P("seq", None, "tp"),
            P(None, "tp"),
            P("seq", None, "tp"),
            P(None, "tp"),
            P("tp", "seq"),
            P("tp"),
            P("seq", "tp"),
            P("tp"),
            P("tp", "seq"),
            P("tp"),
        ),
        check_vma=False,
    )
```

profile of v0, /device:TPU:0, one launch (start us, length us, event | category | flops | bytes accessed | tf_op | source)
XLA Modules:
  0.0 589.2 jit_solution(4795627765267242598)
XLA Ops:
  9.4 2.4 fusion.24
  14.4 2.9 multiply_convert_fusion.4
  17.3 3.5 convolution_add_fusion.4
  21.1 26.5 %all_gather.22 = f32[4,6,1152]{1,0,2:T(4,128)S(1)} all-gather(f32[4,6,288]{1,0,2:T(4,128)S(1)} %copy.102), channel_id=1, replica_groups=mesh['seq'=8,'tp'=4] {'tp'}, dimensions={2}, use_global_device_ids=true | all-gather | bytes 138240 | tf_op jit(solution)/shard_map/all_gather | solution.py:102
  47.6 6.0 %fusion.109 = (f32[4,1,1152]{1,0,2:T(4,128)}, f32[4,1,1152]{1,0,2:T(4,128)}, f32[4,1,1152]{1,0,2:T(4,128)}, f32[4,1,1152]{1,0,2:T(4,128)}) fusion(f32[4,6,1152]{1,0,2:T(4,128)S(1)} %all_gather.22), kind=kLoop, calls=%fused_computation.184 | loop fusion | bytes 147456 | tf_op jit(solution)/shard_map/slice | solution.py:105
  53.6 2.1 copy.105
  55.7 2.3 copy.103
  59.4 3.1 fusion.59
  66.1 3.9 fusion.21
  72.7 6.5 %fusion.113 = (f32[4,640]{1,0:T(4,128)S(1)}, f32[4,640,640]{1,2,0:T(8,128)}) fusion(pred[640,640]{0,1:T(8,128)(4,1)} %broadcast_compare_fusion, bf16[640,4,72]{0,2,1:T(8,128)(2,1)S(1)} %bitcast.99, bf16[640,4,72]{0,2,1:T(8,128)(2,1)S(1)} %bitcast.97), kind=kOutput, calls=%fused_computation.188 | convolution fusion | flops 242483840 | bytes 7710720 | tf_op jit(solution)/shard_map/sub | solution.py:150
  79.2 3.7 fusion.38
  83.7 2.2 convolution_convert_fusion.5
  85.9 2.7 convert_reduce_fusion.4
  88.8 25.1 %reduce-scatter.9.cloned.1.call-done = bf16[640,288]{0,1:T(8,128)(2,1)} async-done(((bf16[640,1152]{0,1:T(8,128)(2,1)}), bf16[640,288]{0,1:T(8,128)(2,1)}) %reduce-scatter.9.cloned.1.call-update) | async-done | bytes 368656 | tf_op jit(solution)/shard_map/reduce_scatter | solution.py:79
  113.9 2.9 fusion.78
  116.9 2.1 copy.111
  119.0 2.3 copy.109
  121.3 3.1 fusion.57
  124.4 10.8 %all-gather.10.cloned.1.call-done = bf16[640,1152]{0,1:T(8,128)(2,1)} async-done(((bf16[640,288]{0,1:T(8,128)(2,1)}), bf16[640,1152]{0,1:T(8,128)(2,1)}) %all-gather.10.cloned.1.call-update) | async-done | bytes 1474576 | tf_op jit(solution)/shard_map/all_gather | solution.py:76
  135.2 6.1 %fusion.115 = f32[640,1152]{0,1:T(8,128)} fusion(bf16[1152,1152]{1,0:T(8,128)(2,1)} %param.32, bf16[640,1152]{0,1:T(8,128)(2,1)} %all-gather.10.cloned.1.call-done), kind=kOutput, calls=%fused_computation.190 | convolution fusion | flops 1698693120 | bytes 7077888 | tf_op jit(solution)/shard_map/rd,fd->rf/dot_general | solution.py:180
  141.3 15.1 %all-gather.8.cloned.1.call-done = bf16[640,1152]{0,1:T(8,128)(2,1)} async-done(((bf16[640,288]{0,1:T(8,128)(2,1)}), bf16[640,1152]{0,1:T(8,128)(2,1)}) %all-gather.8.cloned.1.call-update) | async-done | bytes 1474576 | tf_op jit(solution)/shard_map/all_gather | solution.py:76
  160.0 3.9 fusion.11
  164.0 6.0 %convert_reduce_fusion.2 = (f32[1152]{0:T(1024)S(1)}, bf16[640,1152]{0,1:T(8,128)(2,1)S(1)}, f32[640,1152]{0,1:T(8,128)}) fusion(f32[640,1152]{0,1:T(8,128)S(1)} %copy-done.43, f32[1152]{0:T(1024)S(1)} %convert_element_type.178, bf16[640,1152]{0,1:T(8,128)(2,1)S(1)} %fusion.11, bf16[1152,1152]{1,0:T(8,128)(2,1)S(1)} %copy-done), kind=kOutput, calls=%fused_computation.42 | convolution fusion | flops 1715649408 | bytes 11510784 | tf_op jit(solution)/shard_map/dot_general | solution.py:166
  171.2 4.0 convolution_convert_fusion.3
  175.2 3.4 fusion.4
  178.6 24.3 %reduce-scatter.13.cloned.1.call-done = bf16[640,288]{0,1:T(8,128)(2,1)} async-done(((bf16[640,1152]{0,1:T(8,128)(2,1)}), bf16[640,288]{0,1:T(8,128)(2,1)}) %reduce-scatter.13.cloned.1.call-update) | async-done | bytes 368656 | tf_op jit(solution)/shard_map/reduce_scatter | solution.py:79
  204.3 5.9 all-reduce.1
  210.2 2.9 convert_reduce_fusion.5
  213.2 6.6 %convolution_convert_fusion.4 = bf16[640,1152]{0,1:T(8,128)(2,1)} fusion(bf16[1152,1152]{1,0:T(8,128)(2,1)} %param.32, f32[640,1152]{0,1:T(8,128)} %get-tuple-element.54), kind=kOutput, calls=%fused_computation.28 | convolution fusion | flops 1706065920 | bytes 7077888 | tf_op jit(solution)/shard_map/dot_general | solution.py:171
  219.8 5.4 convolution_convert_fusion.1
  225.3 5.8 convolution_convert_fusion
  231.4 2.1 all-gather.12.cloned.1.call-done
  233.5 2.4 convolution_convert_fusion.7
  237.9 4.1 multiply_reduce_fusion
  247.9 4.3 fusion.41
  252.2 3.2 fusion.9
  257.7 5.6 convolution_convert_fusion.2
  263.7 3.2 fusion.35
  267.2 71.5 %reduce-scatter.21.cloned.1.call-done = bf16[144,1152]{1,0:T(8,128)(2,1)} async-done(((bf16[1152,1152]{1,0:T(8,128)(2,1)}), bf16[144,1152]{1,0:T(8,128)(2,1)}) %reduce-scatter.21.cloned.1.call-update) | async-done | bytes 331792 | tf_op jit(solution)/shard_map/reduce_scatter | solution.py:293
  340.5 71.4 %reduce-scatter.23.cloned.1.call-done = bf16[1152,144]{0,1:T(8,128)(2,1)} async-done(((bf16[1152,1152]{0,1:T(8,128)(2,1)}), bf16[1152,144]{0,1:T(8,128)(2,1)}) %reduce-scatter.23.cloned.1.call-update) | async-done | bytes 331792 | tf_op jit(solution)/shard_map/reduce_scatter | solution.py:294
  413.8 62.3 %reduce-scatter.19.cloned.1.call-done = bf16[288,144]{0,1:T(8,128)(2,1)} async-done(((bf16[288,1152]{0,1:T(8,128)(2,1)}), bf16[288,144]{0,1:T(8,128)(2,1)}) %reduce-scatter.19.cloned.1.call-update) | async-done | bytes 82960 | tf_op jit(solution)/shard_map/reduce_scatter | solution.py:292
  477.7 27.7 %reduce-scatter.15.cloned.1.call-done = bf16[640,288]{0,1:T(8,128)(2,1)} async-done(((bf16[640,1152]{0,1:T(8,128)(2,1)}), bf16[640,288]{0,1:T(8,128)(2,1)}) %reduce-scatter.15.cloned.1.call-update) | async-done | bytes 368656 | tf_op jit(solution)/shard_map/reduce_scatter | solution.py:79
  509.6 2.3 fusion.64
  512.1 31.6 %all-gather = f32[73728]{0:T(1024)S(1)} all-gather(f32[9216]{0:T(1024)S(1)} %concatenate.21), channel_id=2, replica_groups=mesh['seq'=8,'tp'=4] {'seq'}, dimensions={0}, use_global_device_ids=true | all-gather | bytes 331776 | tf_op jit(solution)/shard_map/all_gather | solution.py:253
  548.1 11.1 %all-reduce = (f32[640]{0:T(1024)S(1)}, f32[640]{0:T(1024)S(1)}, f32[32,144]{1,0:T(8,128)S(1)}) all-reduce(f32[640]{0:T(1024)S(1)} %broadcast_multiply_fusion, f32[640]{0:T(1024)S(1)} %broadcast_multiply_fusion.1, f32[32,144]{1,0:T(8,128)S(1)} %convolution_bitcast_fusion.1), channel_id=1, replica_groups=mesh['seq'=8,'tp'=4] {'tp'}, use_global_device_ids=true, to_apply=%region_22.23 | all-reduce | flops 5888 | bytes 47104 | tf_op jit(solution)/shard_map/psum | solution.py:114
  559.9 2.1 fusion.73
  563.9 3.5 fusion.34
  567.3 12.9 %reduce-scatter.17.cloned.1.call-done = bf16[144,3,288]{2,0,1:T(8,128)(2,1)} async-done(((bf16[1152,3,288]{2,0,1:T(8,128)(2,1)}), bf16[144,3,288]{2,0,1:T(8,128)(2,1)}) %reduce-scatter.17.cloned.1.call-update) | async-done | bytes 248848 | tf_op jit(solution)/shard_map/reduce_scatter | solution.py:291
  (186 shorter events, 49.3 us)
Async XLA Ops:
  7.2 156.8 %copy-start = (bf16[1152,1152]{1,0:T(8,128)(2,1)S(1)}, bf16[1152,1152]{1,0:T(8,128)(2,1)}, u32[]{:S(2)}) copy-start(bf16[1152,1152]{1,0:T(8,128)(2,1)} %param.30) | copy-start | bytes 7962628
  7.2 55.3 %all-gather.6.cloned.1.call-start = ((), (), s32[]{:S(2)}) async-start(), calls=%async_computation.8 | async-start | bytes 1843200 | tf_op jit(solution)/shard_map/all_gather | solution.py:76
  9.3 4.4 copy-start.37
  9.3 4.7 copy-start.38
  9.3 4.7 copy-start.27
  9.3 5.1 copy-start.29
  13.7 100.2 %reduce-scatter.9.cloned.1.call-start = ((), (), s32[]{:S(2)}) async-start(), calls=%async_computation.9 | async-start | bytes 1843200 | tf_op jit(solution)/shard_map/reduce_scatter | solution.py:79
  53.6 4.6 copy-start.26
  62.5 3.6 copy-start.2
  66.1 3.9 copy-start.32
  72.7 6.5 %copy-start.16 = (bf16[640,1,288]{0,2,1:T(8,128)(2,1)}, bf16[640,1,288]{0,2,1:T(8,128)(2,1)S(1)}, u32[]{:S(2)}) copy-start(bf16[640,1,288]{0,2,1:T(8,128)(2,1)S(1)} %get-tuple-element.38) | copy-start | bytes 1105924
  72.7 6.5 %copy-start.17 = (bf16[640,1,288]{0,2,1:T(8,128)(2,1)}, bf16[640,1,288]{0,2,1:T(8,128)(2,1)S(1)}, u32[]{:S(2)}) copy-start(bf16[640,1,288]{0,2,1:T(8,128)(2,1)S(1)} %get-tuple-element.39) | copy-start | bytes 1105924
  79.2 4.5 copy-start.36
  83.7 5.1 copy-start.30
  85.9 31.0 %copy-start.28 = (bf16[1152]{0:T(1024)(128)(2,1)S(1)}, bf16[1152]{0:T(1024)(128)(2,1)}, u32[]{:S(2)}) copy-start(bf16[1152]{0:T(1024)(128)(2,1)} %param.31) | copy-start | bytes 6916
  85.9 49.3 %all-gather.10.cloned.1.call-start = ((), (), s32[]{:S(2)}) async-start(), calls=%async_computation.12 | async-start | bytes 1843200 | tf_op jit(solution)/shard_map/all_gather | solution.py:76
  88.7 67.7 %all-gather.8.cloned.1.call-start = ((), (), s32[]{:S(2)}) async-start(), calls=%async_computation.10 | async-start | bytes 1843200 | tf_op jit(solution)/shard_map/all_gather | solution.py:76
  116.8 86.1 %reduce-scatter.13.cloned.1.call-start = ((), (), s32[]{:S(2)}) async-start(), calls=%async_computation.13 | async-start | bytes 1843200 | tf_op jit(solution)/shard_map/reduce_scatter | solution.py:79
  156.4 3.6 copy-start.4
  160.0 4.0 copy-start.43
  164.0 6.0 %copy-start.12 = (bf16[640,1152]{0,1:T(8,128)(2,1)}, bf16[640,1152]{0,1:T(8,128)(2,1)S(1)}, u32[]{:S(2)}) copy-start(bf16[640,1152]{0,1:T(8,128)(2,1)S(1)} %fusion.11) | copy-start | bytes 4423684
  175.2 27.7 %copy-start.5 = (f32[640,1152]{0,1:T(8,128)S(1)}, f32[640,1152]{0,1:T(8,128)}, u32[]{:S(2)}) copy-start(f32[640,1152]{0,1:T(8,128)} %fusion.57) | copy-start | bytes 8847364
  175.2 58.3 %all-gather.12.cloned.1.call-start = ((), (), s32[]{:S(2)}) async-start(), calls=%async_computation.14 | async-start | bytes 1843200 | tf_op jit(solution)/shard_map/all_gather | solution.py:76
  213.1 50.6 %reduce-scatter.11.cloned.1.call-start = ((), (), s32[]{:S(2)}) async-start(), calls=%async_computation.11 | async-start | bytes 1843200 | tf_op jit(solution)/shard_map/reduce_scatter | solution.py:79
  213.2 6.7 %copy-start.13 = (bf16[640,1152]{0,1:T(8,128)(2,1)S(1)}, bf16[640,1152]{0,1:T(8,128)(2,1)}, u32[]{:S(2)}) copy-start(bf16[640,1152]{0,1:T(8,128)(2,1)} %copy-done.12) | copy-start | bytes 4423684
  219.8 5.6 copy-start.34
  219.8 118.9 %reduce-scatter.21.cloned.1.call-start = ((), (), s32[]{:S(2)}) async-start(), calls=%async_computation.18 | async-start | bytes 2985984 | tf_op jit(solution)/shard_map/reduce_scatter | solution.py:293
  225.3 186.7 %reduce-scatter.23.cloned.1.call-start = ((), (), s32[]{:S(2)}) async-start(), calls=%async_computation.19 | async-start | bytes 2985984 | tf_op jit(solution)/shard_map/reduce_scatter | solution.py:294
  231.2 4.7 copy-start.40
  231.2 244.9 %reduce-scatter.19.cloned.1.call-start = ((), (), s32[]{:S(2)}) async-start(), calls=%async_computation.17 | async-start | bytes 995328 | tf_op jit(solution)/shard_map/reduce_scatter | solution.py:292
  235.9 6.1 %copy-start.41 = (bf16[640,288]{0,1:T(8,128)(2,1)}, bf16[640,288]{0,1:T(8,128)(2,1)S(1)}, u32[]{:S(2)}) copy-start(bf16[640,288]{0,1:T(8,128)(2,1)S(1)} %convolution_convert_fusion.7) | copy-start | bytes 1105924
  237.9 4.3 slice-start
  237.9 5.1 slice-start.1
  246.0 259.4 %reduce-scatter.15.cloned.1.call-start = ((), (), s32[]{:S(2)}) async-start(), calls=%async_computation.15 | async-start | bytes 1843200 | tf_op jit(solution)/shard_map/reduce_scatter | solution.py:79
  247.8 4.4 copy-start.20
  247.8 4.4 copy-start.19
  247.8 4.4 copy-start.33
  252.2 3.3 copy-start.24
  252.2 3.5 copy-start.31
  252.2 3.5 copy-start.3
  255.5 324.8 %reduce-scatter.17.cloned.1.call-start = ((), (), s32[]{:S(2)}) async-start(), calls=%async_computation.16 | async-start | bytes 2985984 | tf_op jit(solution)/shard_map/reduce_scatter | solution.py:291
  257.7 6.0 %copy-start.7 = (f32[640,576]{0,1:T(8,128)S(1)}, f32[640,576]{0,1:T(8,128)}, u32[]{:S(2)}) copy-start(f32[640,576]{0,1:T(8,128)} %copy-done.6) | copy-start | bytes 4423684
  257.7 6.0 %copy-start.10 = (f32[640,288]{0,1:T(8,128)S(1)}, f32[640,288]{0,1:T(8,128)}, u32[]{:S(2)}) copy-start(f32[640,288]{0,1:T(8,128)} %get-tuple-element.52) | copy-start | bytes 2211844
  257.7 6.0 %copy-start.14 = (bf16[640,288]{0,1:T(8,128)(2,1)S(1)}, bf16[640,288]{0,1:T(8,128)(2,1)}, u32[]{:S(2)}) copy-start(bf16[640,288]{0,1:T(8,128)(2,1)} %reduce-scatter.9.cloned.1.call-done) | copy-start | bytes 1105924
  267.2 240.9 %copy-start.9 = (f32[640,288]{0,1:T(8,128)S(1)}, f32[640,288]{0,1:T(8,128)}, u32[]{:S(2)}) copy-start(f32[640,288]{0,1:T(8,128)} %get-tuple-element.30) | copy-start | bytes 2211844
  413.8 94.4 %copy-start.8 = (bf16[640,288]{0,1:T(8,128)(2,1)S(1)}, bf16[640,288]{0,1:T(8,128)(2,1)}, u32[]{:S(2)}) copy-start(bf16[640,288]{0,1:T(8,128)(2,1)} %reduce-scatter.13.cloned.1.call-done) | copy-start | bytes 1105924
  543.7 20.1 %copy-start.15 = (bf16[640,288]{0,1:T(8,128)(2,1)S(1)}, bf16[640,288]{0,1:T(8,128)(2,1)}, u32[]{:S(2)}) copy-start(bf16[640,288]{0,1:T(8,128)(2,1)} %reduce-scatter.15.cloned.1.call-done) | copy-start | bytes 1105924
  562.0 20.1 %copy-start.1 = (bf16[1152,1152]{1,0:T(8,128)(2,1)S(1)}, bf16[1152,1152]{1,0:T(8,128)(2,1)}, u32[]{:S(2)}) copy-start(bf16[1152,1152]{1,0:T(8,128)(2,1)} %param.30) | copy-start | bytes 7962628
  (11 other events, 18.8 us)
Sparse Core Ops, SparseCore 0:
  13.8 29.6 all-gather.5
  86.0 27.8 reduce-scatter.8
  116.1 19.0 all-gather.9
  137.3 19.0 all-gather.7
  175.3 27.5 reduce-scatter.12
  213.2 20.2 all-gather.11
  236.1 27.5 reduce-scatter.10
  267.8 70.8 reduce-scatter.20
  342.4 69.5 reduce-scatter.22
  416.2 59.8 reduce-scatter.18
  478.9 26.4 reduce-scatter.14
  508.9 71.3 reduce-scatter.16
where the time goes:
time: 595 us; the launch traced here: 589 us
  waiting for transfers between devices  324 us (54%)
  matrix products  117 us (20%)
  blocking collectives  75 us (13%)
  other arithmetic  33.7 us (6%)
  local copies, waits for them, and re-layouts  23.8 us (4%)
  between operations  15.1 us (3%)
    reduce_scatter x4, waiting for transfers between devices, column_sum(): lax.psum_scatter(part_rows.astype(bf16), 'tp', scatter_dimension=1, tiled...  77.5 us
    reduce_scatter x1, waiting for transfers between devices, local(): lax.psum_scatter(hidden_weight_term, 'seq', scatter_dimension=0, tiled=True)  71.5 us
    reduce_scatter x1, waiting for transfers between devices, local(): lax.psum_scatter(output_weight_term, 'seq', scatter_dimension=1, tiled=True)  71.4 us
    reduce_scatter x1, waiting for transfers between devices, local(): lax.psum_scatter(proj_weight_term, 'seq', scatter_dimension=1, tiled=True)  62.3 us
    all_gather x1, blocking collectives, local(): small_all = lax.all_gather(small, 'seq', axis=0)  31.6 us
    all_gather x4, waiting for transfers between devices, whole_rows(): return lax.all_gather(part_rows, 'tp', axis=1, tiled=True)  28 us
    all_gather x1, blocking collectives, local(): mod_full = lax.all_gather(mod_own, 'tp', axis=2, tiled=True)  26.5 us
    dot_general x6, matrix products, exact_dot(): jnp.dot(left_mat, right_mat, precision=HIGHEST, preferred_element_type=jn...  19.7 us
  transfers between devices with their start and end apart: 12, of which 11 were waited for; matrix products, arithmetic and copies ran while one was open for 20% of the time, Pallas kernels for 0%

commit v1 on v0

--- a/solution.py
+++ b/solution.py
@@ -9,6 +9,28 @@
 ROWS = 640
 NORM_EPS = 1e-06
 HIGHEST = lax.Precision.HIGHEST
+
+
+def laid_out(parts, dim):
+    parts = jnp.moveaxis(parts, 0, dim)
+    dims = parts.shape
+    return parts.reshape(*dims[:dim], dims[dim] * dims[dim + 1], *dims[dim + 2 :])
+
+
+def ring_gather(x, axis, dim):
+    devices = lax.axis_size(axis)
+    pairs = [(i, (i + 1) % devices) for i in range(devices)]
+    back = [(b, a) for a, b in pairs]
+    lower, upper = ([], [])
+    for step in range(devices - 1):
+        if step % 2 == 0:
+            lower.append(lax.ppermute(lower[-1] if lower else x, axis, pairs))
+        else:
+            upper.append(lax.ppermute(upper[-1] if upper else x, axis, back))
+    blocks = jnp.stack([*lower[::-1], x, *upper])
+    shift = lax.axis_index(axis) - len(lower)
+    blocks = blocks[(jnp.arange(devices) - shift) % devices]
+    return laid_out(blocks, dim)
 
 
 def exact_dot(left_mat, right_mat):
@@ -73,7 +95,7 @@
     row_onehot = (row_image[:, None] == jnp.arange(IMG_DEV, dtype=jnp.int32)[None, :]).astype(f32)
 
     def whole_rows(part_rows):
-        return lax.all_gather(part_rows, "tp", axis=1, tiled=True)
+        return ring_gather(part_rows, "tp", 1)
 
     def column_sum(part_rows):
         return lax.psum_scatter(

time: 595 us -> 567 us (0.953)
  waiting for transfers between devices: 324 us -> 277 us
  local copies, waits for them, and re-layouts: 23.8 us -> 41.5 us
  matrix products: 117 us -> 107 us
  starting transfers between devices: 0.88 us -> 10 us
  other arithmetic: 33.7 us -> 42.6 us
  blocking collectives: 75 us -> 67.1 us
    reduce_scatter x1, waiting for transfers between devices: 62.3 us -> 19.7 us  [local(): lax.psum_scatter(proj_weight_term, 'seq', scatter_dimension=1, tiled=True)]
    all_gather x4 -> x0, waiting for transfers between devices: 28 us -> none  [whole_rows(): return lax.all_gather(part_rows, 'tp', axis=1, tiled=True)]
    ppermute x0 -> x12, waiting for transfers between devices: none -> 27.8 us  [the longest x8 27.2 us: ring_gather(): lower.append(lax.ppermute(lower[-1] if lower else x, axis, pairs))]
    gather x0 -> x4, local copies, waits for them, and re-layouts: none -> 13.1 us  [ring_gather(): blocks = blocks[(jnp.arange(devices) - shift) % devices]]
    ppermute x0 -> x12, starting transfers between devices: none -> 9.29 us  [the longest x4 7.14 us: ring_gather(): upper.append(lax.ppermute(upper[-1] if upper else x, axis, back))]
    another operation x3 -> x7, other arithmetic: 1.32 us -> 10.6 us  [the longest x4 9.24 us: ring_gather(): blocks = jnp.stack([*lower[::-1], x, *upper])]
    all_gather x1, blocking collectives: 26.5 us -> 18 us  [local(): mod_full = lax.all_gather(mod_own, 'tp', axis=2, tiled=True)]
  transfers between devices with their start and end apart: 12 -> 20, of which waited for: 11 -> 13; matrix products, arithmetic and copies ran while one was open for 20% -> 23% of each run, Pallas kernels for 0% -> 0%
where the time goes in v1:
time: 567 us; the launch traced here: 561 us
  waiting for transfers between devices  277 us (49%)
  matrix products  107 us (19%)
  blocking collectives  67.1 us (12%)
  other arithmetic  42.6 us (8%)
  local copies, waits for them, and re-layouts  41.5 us (7%)
  between operations  15.2 us (3%)
  starting transfers between devices  10 us (2%)
    reduce_scatter x4, waiting for transfers between devices, column_sum(): lax.psum_scatter(part_rows.astype(bf16), 'tp', scatter_dimension=1, tiled...  73.9 us
    reduce_scatter x1, waiting for transfers between devices, local(): lax.psum_scatter(output_weight_term, 'seq', scatter_dimension=1, tiled=True)  71.7 us
    reduce_scatter x1, waiting for transfers between devices, local(): lax.psum_scatter(hidden_weight_term, 'seq', scatter_dimension=0, tiled=True)  71.3 us
    all_gather x1, blocking collectives, local(): small_all = lax.all_gather(small, 'seq', axis=0)  31.7 us
    ppermute x8, waiting for transfers between devices, ring_gather(): lower.append(lax.ppermute(lower[-1] if lower else x, axis, pairs))  27.2 us
    reduce_scatter x1, waiting for transfers between devices, local(): lax.psum_scatter(proj_weight_term, 'seq', scatter_dimension=1, tiled=True)  19.7 us
    all_gather x1, blocking collectives, local(): mod_full = lax.all_gather(mod_own, 'tp', axis=2, tiled=True)  18 us
    psum x2, blocking collectives, input_grads(): lax.psum((jnp.sum(scaled_grad, axis=1, keepdims=True) / model_width, jnp....  17.4 us
  transfers between devices with their start and end apart: 20, of which 13 were waited for; matrix products, arithmetic and copies ran while one was open for 23% of the time, Pallas kernels for 0%

profile of v1, /device:TPU:0, one launch (start us, length us, event | category | flops | bytes accessed | tf_op | source)
XLA Modules:
  0.0 560.6 jit_solution(2905351657933143893)
XLA Ops:
  9.9 2.4 fusion.20
  20.7 3.5 convolution_add_fusion.4
  24.5 18.0 %all_gather.9 = f32[4,6,1152]{1,0,2:T(4,128)S(1)} all-gather(f32[4,6,288]{1,0,2:T(4,128)S(1)} %copy.102), channel_id=1, replica_groups=mesh['seq'=8,'tp'=4] {'tp'}, dimensions={2}, use_global_device_ids=true | all-gather | bytes 138240 | tf_op jit(solution)/shard_map/all_gather | solution.py:124
  42.5 6.0 %fusion.107 = (f32[4,1,1152]{1,0,2:T(4,128)}, f32[4,1,1152]{1,0,2:T(4,128)}, f32[4,1,1152]{1,0,2:T(4,128)}, f32[4,1,1152]{1,0,2:T(4,128)}) fusion(f32[4,6,1152]{1,0,2:T(4,128)S(1)} %all_gather.9), kind=kLoop, calls=%fused_computation.197 | loop fusion | bytes 147456 | tf_op jit(solution)/shard_map/slice | solution.py:127
  54.7 3.0 fusion.55
  57.7 3.7 collective-permute-done.1
  61.5 2.5 pad_maximum_fusion
  63.9 3.2 gather_fusion
  76.6 7.0 %fusion.111 = (f32[4,640]{1,0:T(4,128)}, f32[4,640,640]{1,2,0:T(8,128)}) fusion(pred[640,640]{0,1:T(8,128)(4,1)} %broadcast_compare_fusion, bf16[640,4,72]{0,2,1:T(8,128)(2,1)S(1)} %bitcast.141, bf16[640,4,72]{0,2,1:T(8,128)(2,1)S(1)} %bitcast.139), kind=kOutput, calls=%fused_computation.201 | convolution fusion | flops 242483840 | bytes 7710720 | tf_op jit(solution)/shard_map/sub | solution.py:172
  83.6 3.6 fusion.34
  90.3 3.3 convert_reduce_fusion.4
  93.6 24.6 %reduce-scatter.9.cloned.1.call-done = bf16[640,288]{0,1:T(8,128)(2,1)} async-done(((bf16[640,1152]{0,1:T(8,128)(2,1)}), bf16[640,288]{0,1:T(8,128)(2,1)}) %reduce-scatter.9.cloned.1.call-update) | async-done | bytes 368656 | tf_op jit(solution)/shard_map/reduce_scatter | solution.py:101
  118.2 2.7 fusion.74
  123.9 2.7 copy.111
  126.7 2.7 copy.109
  131.7 3.8 fusion.53
  135.6 3.2 collective-permute-done.7
  138.8 2.7 pad_maximum_fusion.2
  141.4 3.3 gather_fusion.2
  144.7 2.7 pad_maximum_fusion.1
  147.4 3.2 gather_fusion.1
  158.2 2.6 convolution_add_fusion.2
  160.9 4.2 convert_reduce_fusion
  166.2 3.9 convolution_convert_fusion.3
  170.2 5.6 %convolution_convert_fusion.4 = bf16[640,1152]{0,1:T(8,128)(2,1)} fusion(bf16[1152,1152]{1,0:T(8,128)(2,1)S(1)} %copy-done, f32[640,1152]{0,1:T(8,128)} %copy-done.56), kind=kOutput, calls=%fused_computation.24 | convolution fusion | flops 1706065920 | bytes 7077888 | tf_op jit(solution)/shard_map/dot_general | solution.py:193
  175.9 21.7 %reduce-scatter.13.cloned.1.call-done = bf16[640,288]{0,1:T(8,128)(2,1)} async-done(((bf16[640,1152]{0,1:T(8,128)(2,1)}), bf16[640,288]{0,1:T(8,128)(2,1)}) %reduce-scatter.13.cloned.1.call-update) | async-done | bytes 368656 | tf_op jit(solution)/shard_map/reduce_scatter | solution.py:101
  199.3 5.9 %all-reduce.1 = (f32[640]{0:T(1024)S(1)}, f32[640]{0:T(1024)S(1)}) all-reduce(f32[640]{0:T(1024)S(1)} %get-tuple-element.56, f32[640]{0:T(1024)S(1)} %get-tuple-element.57), channel_id=1, replica_groups=mesh['seq'=8,'tp'=4] {'tp'}, use_global_device_ids=true, to_apply=%region_16.17 | all-reduce | flops 1280 | bytes 10240 | tf_op jit(solution)/shard_map/psum | solution.py:136
  208.8 7.1 %collective-permute-done.9 = bf16[640,288]{0,1:T(8,128)(2,1)S(1)} collective-permute-done((bf16[640,288]{0,1:T(8,128)(2,1)S(1)}, bf16[640,288]{0,1:T(8,128)(2,1)S(1)}, u32[]{:S(2)}, u32[]{:S(2)}) %collective-permute-start.9) | collective-permute-done | bytes 368672 | tf_op jit(solution)/shard_map/ppermute | solution.py:27
  217.3 12.8 %collective-permute-done.10 = bf16[640,288]{0,1:T(8,128)(2,1)S(1)} collective-permute-done((bf16[640,288]{0,1:T(8,128)(2,1)S(1)}, bf16[640,288]{0,1:T(8,128)(2,1)S(1)}, u32[]{:S(2)}, u32[]{:S(2)}) %collective-permute-start.10) | collective-permute-done | bytes 368672 | tf_op jit(solution)/shard_map/ppermute | solution.py:27
  231.5 3.4 gather_fusion.3
  234.9 3.3 convolution_convert_fusion.6
  238.3 6.2 %convolution_convert_fusion = bf16[1152,1152]{0,1:T(8,128)(2,1)} fusion(bf16[640,1152]{0,1:T(8,128)(2,1)} %bitcast.134, f32[640,1152]{0,1:T(8,128)} %copy-done.56), kind=kOutput, calls=%fused_computation.5 | convolution fusion | flops 1706655744 | bytes 7077888 | tf_op jit(solution)/shard_map/rf,rd->fd/dot_general | solution.py:199
  244.6 5.8 %convolution_convert_fusion.1 = bf16[1152,1152]{1,0:T(8,128)(2,1)} fusion(bf16[640,1152]{0,1:T(8,128)(2,1)} %copy-done.17, bf16[640,1152]{0,1:T(8,128)(2,1)} %copy-done.57), kind=kOutput, calls=%fused_computation.6 | convolution fusion | flops 1700020224 | bytes 5603328 | tf_op jit(solution)/shard_map/rd,rf->df/dot_general | solution.py:206
  250.6 2.3 convolution_convert_fusion.7
  253.0 6.9 %multiply_reduce_fusion = (f32[4,640]{1,0:T(4,128)S(1)}, f32[4,640,640]{1,2,0:T(8,128)}) fusion(f32[4,640,640]{1,2,0:T(8,128)} %get-tuple-element.50, f32[4,640]{1,0:T(4,128)S(1)} %copy-done.33, bf16[640,4,72]{0,2,1:T(8,128)(2,1)S(1)} %bitcast.162, bf16[640,4,72]{0,2,1:T(8,128)(2,1)S(1)} %bitcast.150), kind=kOutput, calls=%fused_computation.8 | convolution fusion | flops 240842240 | bytes 13864960 | tf_op jit(solution)/shard_map/qhe,khe->hqk/dot_general | solution.py:227
  259.9 4.0 multiply_convert_fusion
  267.6 3.1 fusion.5
  271.1 5.4 convolution_convert_fusion.2
  277.5 3.1 fusion.31
  280.9 19.7 %reduce-scatter.19.cloned.1.call-done = bf16[288,144]{0,1:T(8,128)(2,1)} async-done(((bf16[288,1152]{0,1:T(8,128)(2,1)}), bf16[288,144]{0,1:T(8,128)(2,1)}) %reduce-scatter.19.cloned.1.call-update) | async-done | bytes 82960 | tf_op jit(solution)/shard_map/reduce_scatter | solution.py:314
  302.3 71.7 %reduce-scatter.23.cloned.1.call-done = bf16[1152,144]{0,1:T(8,128)(2,1)} async-done(((bf16[1152,1152]{0,1:T(8,128)(2,1)}), bf16[1152,144]{0,1:T(8,128)(2,1)}) %reduce-scatter.23.cloned.1.call-update) | async-done | bytes 331792 | tf_op jit(solution)/shard_map/reduce_scatter | solution.py:316
  375.8 71.3 %reduce-scatter.21.cloned.1.call-done = bf16[144,1152]{1,0:T(8,128)(2,1)} async-done(((bf16[1152,1152]{1,0:T(8,128)(2,1)}), bf16[144,1152]{1,0:T(8,128)(2,1)}) %reduce-scatter.21.cloned.1.call-update) | async-done | bytes 331792 | tf_op jit(solution)/shard_map/reduce_scatter | solution.py:315
  449.0 27.5 %reduce-scatter.15.cloned.1.call-done = bf16[640,288]{0,1:T(8,128)(2,1)} async-done(((bf16[640,1152]{0,1:T(8,128)(2,1)}), bf16[640,288]{0,1:T(8,128)(2,1)}) %reduce-scatter.15.cloned.1.call-update) | async-done | bytes 368656 | tf_op jit(solution)/shard_map/reduce_scatter | solution.py:101
  483.4 31.7 %all-gather = f32[73728]{0:T(1024)S(1)} all-gather(f32[9216]{0:T(1024)S(1)} %concatenate.21), channel_id=2, replica_groups=mesh['seq'=8,'tp'=4] {'seq'}, dimensions={0}, use_global_device_ids=true | all-gather | bytes 331776 | tf_op jit(solution)/shard_map/all_gather | solution.py:275
  519.5 11.5 %all-reduce = (f32[640]{0:T(1024)S(1)}, f32[640]{0:T(1024)}, f32[32,144]{1,0:T(8,128)S(1)}) all-reduce(f32[640]{0:T(1024)S(1)} %broadcast_multiply_fusion, f32[640]{0:T(1024)S(1)} %broadcast_multiply_fusion.1, f32[32,144]{1,0:T(8,128)S(1)} %convolution_bitcast_fusion.1), channel_id=1, replica_groups=mesh['seq'=8,'tp'=4] {'tp'}, use_global_device_ids=true, to_apply=%region_22.23 | all-reduce | flops 5888 | bytes 47104 | tf_op jit(solution)/shard_map/psum | solution.py:136
  533.0 2.6 fusion.57
  535.6 3.5 fusion.30
  539.1 12.6 %reduce-scatter.17.cloned.1.call-done = bf16[144,3,288]{2,0,1:T(8,128)(2,1)} async-done(((bf16[1152,3,288]{2,0,1:T(8,128)(2,1)}), bf16[144,3,288]{2,0,1:T(8,128)(2,1)}) %reduce-scatter.17.cloned.1.call-update) | async-done | bytes 248848 | tf_op jit(solution)/shard_map/reduce_scatter | solution.py:313
  (235 shorter events, 77.9 us)
Async XLA Ops:
  7.2 153.7 %copy-start = (bf16[1152,1152]{1,0:T(8,128)(2,1)S(1)}, bf16[1152,1152]{1,0:T(8,128)(2,1)}, u32[]{:S(2)}) copy-start(bf16[1152,1152]{1,0:T(8,128)(2,1)} %param.32) | copy-start | bytes 7962628
  7.2 111.0 %reduce-scatter.9.cloned.1.call-start = ((), (), s32[]{:S(2)}) async-start(), calls=%async_computation.8 | async-start | bytes 1843200 | tf_op jit(solution)/shard_map/reduce_scatter | solution.py:101
  9.9 6.8 %copy-start.52 = (s32[32]{0:T(128)S(1)}, s32[32]{0:T(128)}, u32[]{:S(2)}) copy-start(s32[32]{0:T(128)} %param.20) | copy-start | bytes 388
  9.9 7.1 %copy-start.53 = (s32[32]{0:T(128)S(1)}, s32[32]{0:T(128)}, u32[]{:S(2)}) copy-start(s32[32]{0:T(128)} %param.22) | copy-start | bytes 388
  9.9 7.1 %copy-start.38 = (bf16[2,288]{1,0:T(2,128)(2,1)S(1)}, bf16[2,288]{1,0:T(2,128)(2,1)}, u32[]{:S(2)}) copy-start(bf16[2,288]{1,0:T(2,128)(2,1)} %param.27) | copy-start | bytes 3460
  9.9 7.2 %copy-start.39 = (bf16[6,288]{1,0:T(8,128)(2,1)S(1)}, bf16[6,288]{1,0:T(8,128)(2,1)}, u32[]{:S(2)}) copy-start(bf16[6,288]{1,0:T(8,128)(2,1)} %param.25) | copy-start | bytes 10372
  9.9 8.6 %copy-start.43 = (s32[32]{0:T(128)S(1)}, s32[32]{0:T(128)}, u32[]{:S(2)}) copy-start(s32[32]{0:T(128)} %param.21) | copy-start | bytes 388
  14.3 39.8 %collective-permute-start = (bf16[640,288]{0,1:T(8,128)(2,1)}, bf16[640,288]{0,1:T(8,128)(2,1)}, u32[]{:S(2)}, u32[]{:S(2)}) collective-permute-start(bf16[640,288]{0,1:T(8,128)(2,1)} %slice.142), channel_id=1, source_target_pairs={{0,1},{1,2},{2,3},{3,0},{4,5},{5,6},{6,7},{7,4},{8,9},{9,10},{10,1... | collective-permute-start | bytes 1105928 | tf_op jit(solution)/shard_map/ppermute | solution.py:27
  14.7 43.0 %collective-permute-start.2 = (bf16[640,288]{0,1:T(8,128)(2,1)}, bf16[640,288]{0,1:T(8,128)(2,1)}, u32[]{:S(2)}, u32[]{:S(2)}) collective-permute-start(bf16[640,288]{0,1:T(8,128)(2,1)} %slice.142), channel_id=1, source_target_pairs={{1,0},{2,1},{3,2},{0,3},{5,4},{6,5},{7,6},{4,7},{9,8},{10,9},{11,1... | collective-permute-start | bytes 1105928 | tf_op jit(solution)/shard_map/ppermute | solution.py:29
  20.7 21.8 %copy-start.31 = (bf16[32,1152]{1,0:T(8,128)(2,1)}, bf16[32,1152]{1,0:T(8,128)(2,1)S(1)}, u32[]{:S(2)}) copy-start(bf16[32,1152]{1,0:T(8,128)(2,1)S(1)} %get-tuple-element.47) | copy-start | bytes 221188
  24.2 24.3 %copy-start.30 = (f32[4,6,288]{2,0,1:T(4,128)}, f32[4,6,288]{2,0,1:T(4,128)S(1)}, u32[]{:S(2)}) copy-start(f32[4,6,288]{2,0,1:T(4,128)S(1)} %convolution_add_fusion.4) | copy-start | bytes 82948
  54.1 7.4 %collective-permute-start.1 = (bf16[640,288]{0,1:T(8,128)(2,1)}, bf16[640,288]{0,1:T(8,128)(2,1)S(1)}, u32[]{:S(2)}, u32[]{:S(2)}) collective-permute-start(bf16[640,288]{0,1:T(8,128)(2,1)} %collective-permute-done), channel_id=1, source_target_pairs={{0,1},{1,2},{2,3},{3,0},{4,5},{5,6},{6,7},{7,4},{8,9},{9,10},{10,1... | collective-permute-start | bytes 1105928 | tf_op jit(solution)/shard_map/ppermute | solution.py:27
  54.7 92.7 %copy-start.34 = (s32[1024]{0:T(1024)}, s32[1024]{0:T(1024)S(1)}, u32[]{:S(2)}) copy-start(s32[1024]{0:T(1024)S(1)} %pad_clamp_fusion) | copy-start | bytes 12292
  76.6 7.0 %copy-start.18 = (bf16[640,1,288]{0,2,1:T(8,128)(2,1)}, bf16[640,1,288]{0,2,1:T(8,128)(2,1)S(1)}, u32[]{:S(2)}) copy-start(bf16[640,1,288]{0,2,1:T(8,128)(2,1)S(1)} %get-tuple-element.38) | copy-start | bytes 1105924
  76.6 7.0 %copy-start.20 = (bf16[640,1,288]{0,2,1:T(8,128)(2,1)}, bf16[640,1,288]{0,2,1:T(8,128)(2,1)S(1)}, u32[]{:S(2)}) copy-start(bf16[640,1,288]{0,2,1:T(8,128)(2,1)S(1)} %get-tuple-element.39) | copy-start | bytes 1105924
  83.6 4.4 copy-start.51
  88.0 5.6 copy-start.45
  90.2 107.4 %reduce-scatter.13.cloned.1.call-start = ((), (), s32[]{:S(2)}) async-start(), calls=%async_computation.10 | async-start | bytes 1843200 | tf_op jit(solution)/shard_map/reduce_scatter | solution.py:101
  93.6 29.1 %collective-permute-start.6 = (bf16[640,288]{0,1:T(8,128)(2,1)}, bf16[640,288]{0,1:T(8,128)(2,1)}, u32[]{:S(2)}, u32[]{:S(2)}) collective-permute-start(bf16[640,288]{0,1:T(8,128)(2,1)} %get-tuple-element.25), channel_id=1, source_target_pairs={{0,1},{1,2},{2,3},{3,0},{4,5},{5,6},{6,7},{7,4},{8,9},{9,10},{10,1... | collective-permute-start | bytes 1105928 | tf_op jit(solution)/shard_map/ppermute | solution.py:27
  120.9 10.6 %collective-permute-start.3 = (bf16[640,288]{0,1:T(8,128)(2,1)}, bf16[640,288]{0,1:T(8,128)(2,1)}, u32[]{:S(2)}, u32[]{:S(2)}) collective-permute-start(bf16[640,288]{0,1:T(8,128)(2,1)} %get-tuple-element.51), channel_id=1, source_target_pairs={{0,1},{1,2},{2,3},{3,0},{4,5},{5,6},{6,7},{7,4},{8,9},{9,10},{10,1... | collective-permute-start | bytes 1105928 | tf_op jit(solution)/shard_map/ppermute | solution.py:27
  120.9 14.7 %collective-permute-start.8 = (bf16[640,288]{0,1:T(8,128)(2,1)}, bf16[640,288]{0,1:T(8,128)(2,1)}, u32[]{:S(2)}, u32[]{:S(2)}) collective-permute-start(bf16[640,288]{0,1:T(8,128)(2,1)} %get-tuple-element.25), channel_id=1, source_target_pairs={{1,0},{2,1},{3,2},{0,3},{5,4},{6,5},{7,6},{4,7},{9,8},{10,9},{11,1... | collective-permute-start | bytes 1105928 | tf_op jit(solution)/shard_map/ppermute | solution.py:29
  122.7 16.1 %collective-permute-start.7 = (bf16[640,288]{0,1:T(8,128)(2,1)}, bf16[640,288]{0,1:T(8,128)(2,1)}, u32[]{:S(2)}, u32[]{:S(2)}) collective-permute-start(bf16[640,288]{0,1:T(8,128)(2,1)} %collective-permute-done.6), channel_id=1, source_target_pairs={{0,1},{1,2},{2,3},{3,0},{4,5},{5,6},{6,7},{7,4},{8,9},{9,10},{10,1... | collective-permute-start | bytes 1105928 | tf_op jit(solution)/shard_map/ppermute | solution.py:27
  129.4 15.4 %collective-permute-start.5 = (bf16[640,288]{0,1:T(8,128)(2,1)}, bf16[640,288]{0,1:T(8,128)(2,1)}, u32[]{:S(2)}, u32[]{:S(2)}) collective-permute-start(bf16[640,288]{0,1:T(8,128)(2,1)} %get-tuple-element.51), channel_id=1, source_target_pairs={{1,0},{2,1},{3,2},{0,3},{5,4},{6,5},{7,6},{4,7},{9,8},{10,9},{11,1... | collective-permute-start | bytes 1105928 | tf_op jit(solution)/shard_map/ppermute | solution.py:29
  131.5 13.2 %collective-permute-start.4 = (bf16[640,288]{0,1:T(8,128)(2,1)}, bf16[640,288]{0,1:T(8,128)(2,1)}, u32[]{:S(2)}, u32[]{:S(2)}) collective-permute-start(bf16[640,288]{0,1:T(8,128)(2,1)} %collective-permute-done.3), channel_id=1, source_target_pairs={{0,1},{1,2},{2,3},{3,0},{4,5},{5,6},{6,7},{7,4},{8,9},{9,10},{10,1... | collective-permute-start | bytes 1105928 | tf_op jit(solution)/shard_map/ppermute | solution.py:27
  160.9 4.3 copy-start.56
  170.2 106.4 %reduce-scatter.11.cloned.1.call-start = ((), (), s32[]{:S(2)}) async-start(), calls=%async_computation.9 | async-start | bytes 1843200 | tf_op jit(solution)/shard_map/reduce_scatter | solution.py:101
  175.9 29.3 %copy-start.9 = (f32[640,576]{0,1:T(8,128)S(1)}, f32[640,576]{0,1:T(8,128)}, u32[]{:S(2)}) copy-start(f32[640,576]{0,1:T(8,128)} %copy-done.8) | copy-start | bytes 4423684
  175.9 124.8 %reduce-scatter.19.cloned.1.call-start = ((), (), s32[]{:S(2)}) async-start(), calls=%async_computation.13 | async-start | bytes 995328 | tf_op jit(solution)/shard_map/reduce_scatter | solution.py:314
  207.0 272.2 %copy-start.11 = (f32[640,288]{0,1:T(8,128)}, f32[640,288]{0,1:T(8,128)S(1)}, u32[]{:S(2)}) copy-start(f32[640,288]{0,1:T(8,128)S(1)} %get-tuple-element.30) | copy-start | bytes 2211844
  207.0 8.9 %collective-permute-start.9 = (bf16[640,288]{0,1:T(8,128)(2,1)S(1)}, bf16[640,288]{0,1:T(8,128)(2,1)S(1)}, u32[]{:S(2)}, u32[]{:S(2)}) collective-permute-start(bf16[640,288]{0,1:T(8,128)(2,1)S(1)} %get-tuple-element.29), channel_id=1, source_target_pairs={{0,1},{1,2},{2,3},{3,0},{4,5},{5,6},{6,7},{7,4},{8,9},{9,10},{10,1... | collective-permute-start | bytes 1105928 | tf_op jit(solution)/shard_map/ppermute | solution.py:27
  207.1 10.2 %collective-permute-start.11 = (bf16[640,288]{0,1:T(8,128)(2,1)S(1)}, bf16[640,288]{0,1:T(8,128)(2,1)S(1)}, u32[]{:S(2)}, u32[]{:S(2)}) collective-permute-start(bf16[640,288]{0,1:T(8,128)(2,1)S(1)} %get-tuple-element.29), channel_id=1, source_target_pairs={{1,0},{2,1},{3,2},{0,3},{5,4},{6,5},{7,6},{4,7},{9,8},{10,9},{11,1... | collective-permute-start | bytes 1105928 | tf_op jit(solution)/shard_map/ppermute | solution.py:29
  215.9 14.2 %collective-permute-start.10 = (bf16[640,288]{0,1:T(8,128)(2,1)S(1)}, bf16[640,288]{0,1:T(8,128)(2,1)S(1)}, u32[]{:S(2)}, u32[]{:S(2)}) collective-permute-start(bf16[640,288]{0,1:T(8,128)(2,1)S(1)} %collective-permute-done.9), channel_id=1, source_target_pairs={{0,1},{1,2},{2,3},{3,0},{4,5},{5,6},{6,7},{7,4},{8,9},{9,10},{10,1... | collective-permute-start | bytes 1105928 | tf_op jit(solution)/shard_map/ppermute | solution.py:27
  238.2 135.8 %reduce-scatter.23.cloned.1.call-start = ((), (), s32[]{:S(2)}) async-start(), calls=%async_computation.15 | async-start | bytes 2985984 | tf_op jit(solution)/shard_map/reduce_scatter | solution.py:316
  244.5 202.7 %reduce-scatter.21.cloned.1.call-start = ((), (), s32[]{:S(2)}) async-start(), calls=%async_computation.14 | async-start | bytes 2985984 | tf_op jit(solution)/shard_map/reduce_scatter | solution.py:315
  250.4 226.1 %reduce-scatter.15.cloned.1.call-start = ((), (), s32[]{:S(2)}) async-start(), calls=%async_computation.11 | async-start | bytes 1843200 | tf_op jit(solution)/shard_map/reduce_scatter | solution.py:101
  252.9 6.9 %slice-start = ((s8[6553600]{0:T(1024)(128)(4,1)}), s8[4194304]{0:T(1024)(128)(4,1)S(1)}, s32[]{:S(2)}) async-start(s8[6553600]{0:T(1024)(128)(4,1)} %bitcast.132), calls=%async_computation.16 | async-start | bytes 8388608
  253.0 6.9 %slice-start.1 = ((s8[6553600]{0:T(1024)(128)(4,1)}), s8[2359296]{0:T(1024)(128)(4,1)S(1)}, s32[]{:S(2)}) async-start(s8[6553600]{0:T(1024)(128)(4,1)} %bitcast.132), calls=%async_computation.17 | async-start | bytes 4718592
  259.9 4.0 copy-start.21
  270.8 280.9 %reduce-scatter.17.cloned.1.call-start = ((), (), s32[]{:S(2)}) async-start(), calls=%async_computation.12 | async-start | bytes 2985984 | tf_op jit(solution)/shard_map/reduce_scatter | solution.py:313
  276.6 4.0 copy-start.23
  276.6 4.0 copy-start.25
  276.6 4.0 copy-start.29
  302.3 177.0 %copy-start.15 = (bf16[640,288]{0,1:T(8,128)(2,1)S(1)}, bf16[640,288]{0,1:T(8,128)(2,1)}, u32[]{:S(2)}) copy-start(bf16[640,288]{0,1:T(8,128)(2,1)} %reduce-scatter.9.cloned.1.call-done) | copy-start | bytes 1105924
  449.0 30.4 %copy-start.10 = (bf16[640,288]{0,1:T(8,128)(2,1)S(1)}, bf16[640,288]{0,1:T(8,128)(2,1)}, u32[]{:S(2)}) copy-start(bf16[640,288]{0,1:T(8,128)(2,1)} %reduce-scatter.13.cloned.1.call-done) | copy-start | bytes 1105924
  483.1 48.5 %copy-start.44 = (s32[32]{0:T(128)S(1)}, s32[32]{0:T(128)}, u32[]{:S(2)}) copy-start(s32[32]{0:T(128)} %param.21) | copy-start | bytes 388
  515.2 20.5 %copy-start.12 = (f32[640,288]{0,1:T(8,128)S(1)}, f32[640,288]{0,1:T(8,128)}, u32[]{:S(2)}) copy-start(f32[640,288]{0,1:T(8,128)} %copy-done.11) | copy-start | bytes 2211844
  515.2 20.4 %copy-start.42 = (s32[1024]{0:T(1024)S(1)}, s32[1024]{0:T(1024)}, u32[]{:S(2)}) copy-start(s32[1024]{0:T(1024)} %copy-done.40) | copy-start | bytes 12292
  535.6 17.9 %copy-start.1 = (bf16[1152,1152]{1,0:T(8,128)(2,1)S(1)}, bf16[1152,1152]{1,0:T(8,128)(2,1)}, u32[]{:S(2)}) copy-start(bf16[1152,1152]{1,0:T(8,128)(2,1)} %param.32) | copy-start | bytes 7962628
  (32 other events, 71.8 us)
Sparse Core Ops, SparseCore 0:
  90.4 27.8 reduce-scatter.8
  170.3 27.2 reduce-scatter.12
  200.2 31.4 reduce-scatter.10
  238.3 62.2 reduce-scatter.18
  304.6 69.3 reduce-scatter.22
  377.5 69.6 reduce-scatter.20
  449.9 26.5 reduce-scatter.14
  480.2 71.4 reduce-scatter.16
